TPU v7x, 32 devices: a whole 2x2x4 slice. The times are simulated.
32 devices in a mesh: wide: 4 (over z), narrow: 8 (over y, x, core).
Axes of the slice: x: 2, y: 2, z: 4, core: 2. Of those that a mesh axis runs over, the one named last changes fastest.
Arguments:
- src_design: float32 [5, 4194304], P(None, ('wide', 'narrow')), may hold values from -6 to 6
- att_design: float32 [16, 4194304], P(None, ('wide', 'narrow')), may hold values from -3 to 3
- right_side: float32 [4194304], P(('wide', 'narrow')), may hold values from -6 to 6
- block_source: int32 [65536], P(('wide', 'narrow')), may hold values from 0 to 65535, as said below
- block_segment: int32 [65536], P(('wide', 'narrow')), may hold values from 0 to 8191, as said below
- block_count: int32 [65536], P(('wide', 'narrow')), may hold values from 8 to 64
Outputs:
- sol_src: float32 [5, 65536], P(None, ('wide', 'narrow'))
- sol_att: float32 [16, 8192], P(None, 'narrow')
- dir_src: float32 [5, 65536], P(None, ('wide', 'narrow'))
- dir_att: float32 [16, 8192], P(None, 'narrow')
Inputs may be any that keep to these rules, and one draw needn't show every extreme that they name: `block_source`: A block held by the device at index w of wide names a source in [w * 2048 * 8, (w + 1) * 2048 * 8); of the 2048 blocks of one device, exactly 2048 / 8 name sources in [(w * 8 + m) * 2048, (w * 8 + m + 1) * 2048) for each m in 0 to 8 - 1; the lowest and highest source of the partition are named on every device. `block_segment`: A block held by the device at index n of narrow names a segment in [n * 1024, (n + 1) * 1024); the lowest and highest of that range are named on every device.
All inputs are finite; a program needn't handle non-finite values.
Results may differ from a plain program's by a relative error of at most 0.00018.
Values sent between devices are 32-bit elements; how exact they have to be, the bound alone decides.
No kernel may reach another device: no remote copies, remote signals or barrier semaphores. Data moves between devices by JAX's collectives and lax.ppermute only.
A program may use at most 192 MiB of HBM per device.

v0:
```python
import jax
import jax.numpy as jnp
from jax import lax
from jax.sharding import PartitionSpec as P

ITERS = 2
SRC_DEV = 2048
SEG_DEV = 1024


def on_device(src_design, att_design, right_side, block_source, block_segment, block_count):
    block_total = block_source.shape[0]
    narrow_size = lax.axis_size("narrow")
    group_size = SRC_DEV * narrow_size
    wide_at = lax.axis_index("wide")
    narrow_at = lax.axis_index("narrow")
    src_index = block_source - wide_at * group_size
    seg_index = block_segment - narrow_at * SEG_DEV
    src_blocks = src_design.reshape(src_design.shape[0], block_total, -1)
    att_blocks = att_design.reshape(att_design.shape[0], block_total, -1)
    param_rows = src_blocks.shape[0]
    obs_width = src_blocks.shape[2]
    live_rows = (jnp.arange(obs_width, dtype=jnp.int32)[None, :] < block_count[:, None]).astype(
        jnp.float32
    )
    att_weight = (wide_at == 0).astype(jnp.float32)
    src_weight = jnp.float32(1.0)

    def transposed(obs_vec):
        src_part = jnp.sum(src_blocks * obs_vec[None], axis=2)
        att_part = jnp.sum(att_blocks * obs_vec[None], axis=2)
        att_total = (
            jnp.zeros((att_blocks.shape[0], SEG_DEV), jnp.float32).at[:, seg_index].add(att_part)
        )
        att_vec = lax.psum(att_total, "wide")
        src_total = jnp.zeros((param_rows, group_size), jnp.float32).at[:, src_index].add(src_part)
        src_vec = lax.psum_scatter(src_total, "narrow", scatter_dimension=1, tiled=True)
        return (src_vec, att_vec)

    def param_dot(first_src, first_att, second_src, second_att):
        return src_weight * jnp.sum(first_src * second_src) + att_weight * jnp.sum(
            first_att * second_att
        )

    def merged_total(first, second, third, fourth):
        return lax.psum((first, second, third, fourth), ("wide", "narrow"))

    obs_vec = right_side.reshape(block_total, obs_width) * live_rows
    src_raw, att_raw = transposed(obs_vec)
    zero_val = jnp.float32(0.0)
    totals = merged_total(
        jnp.sum(obs_vec * obs_vec),
        param_dot(src_raw, att_raw, src_raw, att_raw),
        zero_val,
        zero_val,
    )
    beta_norm = jnp.sqrt(totals[0])
    alpha_norm = jnp.sqrt(totals[1]) / beta_norm
    obs_vec = obs_vec / beta_norm
    src_vec = src_raw / beta_norm / alpha_norm
    att_vec = att_raw / beta_norm / alpha_norm
    dir_src, dir_att = (src_vec, att_vec)
    sol_src = jnp.zeros_like(src_vec)
    sol_att = jnp.zeros_like(att_vec)
    phi_bar = beta_norm
    rho_bar = alpha_norm
    for step in range(ITERS):
        whole_src = lax.all_gather(src_vec, "narrow", axis=1, tiled=True)
        src_vals = jnp.take(whole_src, src_index, axis=1)
        att_vals = jnp.take(att_vec, seg_index, axis=1)
        image = jnp.sum(src_blocks * src_vals[:, :, None], axis=0)
        image = image + jnp.sum(att_blocks * att_vals[:, :, None], axis=0)
        obs_raw = image * live_rows - alpha_norm * obs_vec
        src_raw, att_raw = transposed(obs_raw)
        totals = merged_total(
            jnp.sum(obs_raw * obs_raw),
            param_dot(src_raw, att_raw, src_raw, att_raw),
            param_dot(src_raw, att_raw, src_vec, att_vec),
            param_dot(src_vec, att_vec, src_vec, att_vec),
        )
        beta_norm = jnp.sqrt(totals[0])
        alpha_square = (
            totals[1] / (beta_norm * beta_norm)
            - 2.0 * totals[2]
            + beta_norm * beta_norm * totals[3]
        )
        alpha_norm = jnp.sqrt(alpha_square)
        obs_vec = obs_raw / beta_norm
        src_vec = (src_raw / beta_norm - beta_norm * src_vec) / alpha_norm
        att_vec = (att_raw / beta_norm - beta_norm * att_vec) / alpha_norm
        rho_val = jnp.sqrt(rho_bar * rho_bar + beta_norm * beta_norm)
        cosine = rho_bar / rho_val
        sine_part = beta_norm / rho_val
        theta_val = sine_part * alpha_norm
        rho_bar = -cosine * alpha_norm
        phi_val = cosine * phi_bar
        phi_bar = sine_part * phi_bar
        sol_src = sol_src + phi_val / rho_val * dir_src
        sol_att = sol_att + phi_val / rho_val * dir_att
        dir_src = src_vec - theta_val / rho_val * dir_src
        dir_att = att_vec - theta_val / rho_val * dir_att
    return (sol_src, sol_att, dir_src, dir_att)


def solution(mesh):
    in_specs = (
        P(None, ("wide", "narrow")),
        P(None, ("wide", "narrow")),
        P(("wide", "narrow")),
        P(("wide", "narrow")),
        P(("wide", "narrow")),
        P(("wide", "narrow")),
    )
    out_specs = (
        P(None, ("wide", "narrow")),
        P(None, "narrow"),
        P(None, ("wide", "narrow")),
        P(None, "narrow"),
    )
    return jax.shard_map(
        on_device, mesh=mesh, in_specs=in_specs, out_specs=out_specs, check_vma=False
    )
```

profile of v0, /device:TPU:0, one launch (start us, length us, event | category | flops | bytes accessed | tf_op | source)
XLA Modules:
  0.0 607.7 jit_solution(5175881611888121235)
XLA Ops:
  8.1 17.4 %reshape.145 = f32[16,2048,64]{2,1,0:T(8,128)} reshape(f32[16,131072]{1,0:T(8,128)} %param.11) | data formatting | bytes 16777216 | tf_op jit(solution)/shard_map/reshape | solution.py:20
  26.1 8.2 %multiply_reduce_fusion.2 = f32[16,2048]{1,0:T(8,128)S(1)} fusion(f32[16,2048,64]{2,1,0:T(8,128)} %reshape.145, f32[2048,64]{1,0:T(8,128)S(1)} %fusion.6), kind=kLoop, calls=%fused_computation.12 | loop fusion | flops 4161536 | bytes 9043968 | tf_op jit(solution)/shard_map/reduce_sum | solution.py:31
  35.7 12.0 %scatter_custom_fusion.1 = f32[16,1024]{0,1:T(8,128)S(1)} fusion(s32[2048]{0:T(1024)S(1)} %get-tuple-element.45, f32[2048,16]{1,0:T(8,128)} %copy.42, f32[]{:T(128)} %constant.27.clone.1), kind=kCustom, calls=%fused_computation.43 | custom fusion | flops 32768 | bytes 66048 | tf_op jit(solution)/shard_map/scatter-add | solution.py:33
  48.7 6.6 %reshape.143 = f32[5,2048,64]{2,1,0:T(8,128)} reshape(f32[5,131072]{1,0:T(8,128)} %param.10) | data formatting | bytes 5242880 | tf_op jit(solution)/shard_map/reshape | solution.py:19
  55.3 3.9 multiply_reduce_fusion.7
  59.7 15.2 %scatter_custom_fusion = f32[5,16384]{0,1:T(8,128)} fusion(s32[2048]{0:T(1024)S(1)} %get-tuple-element.47, f32[2048,5]{1,0:T(8,128)S(1)} %copy.40, f32[]{:T(128)} %constant.27.clone.1), kind=kCustom, calls=%fused_computation.24 | custom fusion | flops 10240 | bytes 327684 | tf_op jit(solution)/shard_map/scatter-add | solution.py:36
  74.8 6.0 copy.41
  82.4 3.3 all-reduce.7.cloned.1.call-done
  87.8 30.0 %reduce-scatter.4.cloned.1.call-done = f32[5,2048]{1,0:T(8,128)} async-done(((f32[5,16384]{1,0:T(8,128)}), f32[5,2048]{1,0:T(8,128)}) %reduce-scatter.4.cloned.1.call-update) | async-done | bytes 40976 | tf_op jit(solution)/shard_map/reduce_scatter | solution.py:37
  119.9 39.6 %all-reduce.2 = (f32[]{:T(128)}, f32[]{:T(128)}) all-reduce(f32[]{:T(128)} %multiply_reduce_fusion.12, f32[]{:T(128)S(6)} %add.133), channel_id=1, replica_groups=mesh['wide'=4,'narrow'=8] {'wide','narrow'}, use_global_device_ids=true, to_apply=%region_10.0 | all-reduce | flops 2 | bytes 16 | tf_op jit(solution)/shard_map/psum | solution.py:46
  161.7 10.8 %all_gather.6 = f32[5,16384]{1,0:T(8,128)S(1)} all-gather(f32[5,2048]{1,0:T(8,128)S(1)} %broadcast_divide_fusion.1), channel_id=1, replica_groups=mesh['wide'=4,'narrow'=8] {'narrow'}, dimensions={1}, use_global_device_ids=true | all-gather | bytes 368640 | tf_op jit(solution)/shard_map/all_gather | solution.py:68
  172.6 5.7 copy.44
  178.2 11.0 %gather_fusion = f32[2048,5]{1,0:T(8,128)} fusion(f32[5,16384]{0,1:T(8,128)} %copy.44, s32[2048]{0:T(1024)S(1)} %broadcast_clamp_fusion.1), kind=kCustom, calls=%fused_computation.clone | custom fusion | bytes 90112 | tf_op jit(solution)/shard_map/jit(_take)/gather | solution.py:69
  191.1 3.4 mul.345
  194.5 6.1 %mul.346 = f32[5,131072]{1,0:T(8,128)} reshape(f32[5,2048,64]{2,1,0:T(8,128)} %mul.345) | data formatting | bytes 5242880 | tf_op jit(solution)/shard_map/mul | solution.py:71
  200.7 5.8 multiply_reduce_fusion.9
  206.7 7.6 %gather_fusion.1 = f32[2048,16]{1,0:T(8,128)} fusion(f32[16,1024]{0,1:T(8,128)S(1)} %copy.46, s32[2048]{0:T(1024)S(1)} %broadcast_clamp_fusion), kind=kCustom, calls=%fused_computation.1.clone | custom fusion | bytes 270336 | tf_op jit(solution)/shard_map/jit(_take)/gather | solution.py:70
  216.1 8.3 %mul.348 = f32[16,2048,64]{2,1,0:T(8,128)} broadcast(f32[16,2048]{1,0:T(8,128)S(1)} %copy.47), dimensions={0,1} | broadcast | bytes 8519680 | tf_op jit(solution)/shard_map/mul | solution.py:72
  224.4 15.5 %mul.349 = f32[16,131072]{1,0:T(8,128)} reshape(f32[16,2048,64]{2,1,0:T(8,128)} %mul.348) | data formatting | bytes 16777216 | tf_op jit(solution)/shard_map/mul | solution.py:72
  239.9 7.6 %multiply_reduce_fusion.4 = f32[131072]{0:T(1024)S(1)} fusion(f32[16,131072]{1,0:T(8,128)} %param.11, f32[16,131072]{1,0:T(8,128)} %mul.349), kind=kLoop, calls=%fused_computation.14 | loop fusion | flops 4063232 | bytes 17301504 | tf_op jit(solution)/shard_map/reduce_sum | solution.py:72
  251.1 8.4 %multiply_reduce_fusion.1 = f32[16,2048]{1,0:T(8,128)S(1)} fusion(f32[16,2048,64]{2,1,0:T(8,128)} %reshape.145, f32[2048,64]{1,0:T(8,128)S(1)} %multiply_subtract_fusion.1), kind=kLoop, calls=%fused_computation.11 | loop fusion | flops 4161536 | bytes 9043968 | tf_op jit(solution)/shard_map/reduce_sum | solution.py:31
  260.8 12.0 %scatter_custom_fusion.3 = f32[16,1024]{0,1:T(8,128)S(1)} fusion(s32[2048]{0:T(1024)S(1)} %get-tuple-element.45, f32[2048,16]{1,0:T(8,128)} %copy.50, f32[]{:T(128)} %constant.27.clone.1), kind=kCustom, calls=%fused_computation.41 | custom fusion | flops 32768 | bytes 66048 | tf_op jit(solution)/shard_map/scatter-add | solution.py:33
  273.7 3.9 multiply_reduce_fusion.6
  278.0 15.2 %scatter_custom_fusion.2 = f32[5,16384]{0,1:T(8,128)} fusion(s32[2048]{0:T(1024)S(1)} %get-tuple-element.47, f32[2048,5]{1,0:T(8,128)S(1)} %copy.48, f32[]{:T(128)} %constant.27.clone.1), kind=kCustom, calls=%fused_computation.22 | custom fusion | flops 10240 | bytes 327684 | tf_op jit(solution)/shard_map/scatter-add | solution.py:36
  293.2 6.0 copy.49
  299.2 7.9 %all-reduce.9.cloned.1.call-done = f32[16,1024]{1,0:T(8,128)} async-done(((f32[16,1024]{1,0:T(8,128)}), f32[16,1024]{1,0:T(8,128)}) %all-reduce.9.cloned.1.call-update) | async-done | bytes 65552 | tf_op jit(solution)/shard_map/psum | solution.py:35
  310.5 21.9 %reduce-scatter.6.cloned.1.call-done = f32[5,2048]{1,0:T(8,128)} async-done(((f32[5,16384]{1,0:T(8,128)}), f32[5,2048]{1,0:T(8,128)}) %reduce-scatter.6.cloned.1.call-update) | async-done | bytes 40976 | tf_op jit(solution)/shard_map/reduce_scatter | solution.py:37
  335.9 39.6 %all-reduce.1 = (f32[]{:T(128)}, f32[]{:T(128)}, f32[]{:T(128)}, f32[]{:T(128)}) all-reduce(f32[]{:T(128)S(6)} %add.137, f32[]{:T(128)} %get-tuple-element.42, f32[]{:T(128)S(6)} %add.138, f32[]{:T(128)S(6)} %add.139), channel_id=1, replica_groups=mesh['wide'=4,'narrow'=8] {'wide','narrow'}, use_global_device_ids=true, to_apply=%region_23.26 | all-reduce | flops 4 | bytes 32 | tf_op jit(solution)/shard_map/psum | solution.py:46
  379.1 7.6 %gather_fusion.3 = f32[2048,16]{1,0:T(8,128)} fusion(f32[16,1024]{0,1:T(8,128)S(1)} %copy.54, s32[2048]{0:T(1024)S(1)} %broadcast_clamp_fusion), kind=kCustom, calls=%fused_computation.3.clone | custom fusion | bytes 270336 | tf_op jit(solution)/shard_map/jit(_take)/gather | solution.py:70
  389.2 9.2 %mul.384 = f32[16,2048,64]{2,1,0:T(8,128)} broadcast(f32[16,2048]{1,0:T(8,128)} %copy.55), dimensions={0,1} | broadcast | bytes 8519680 | tf_op jit(solution)/shard_map/mul | solution.py:72
  398.4 15.5 %mul.385 = f32[16,131072]{1,0:T(8,128)} reshape(f32[16,2048,64]{2,1,0:T(8,128)} %mul.384) | data formatting | bytes 16777216 | tf_op jit(solution)/shard_map/mul | solution.py:72
  413.9 8.2 %multiply_reduce_fusion.3 = f32[131072]{0:T(1024)} fusion(f32[16,131072]{1,0:T(8,128)} %param.11, f32[16,131072]{1,0:T(8,128)} %mul.385), kind=kLoop, calls=%fused_computation.13 | loop fusion | flops 4063232 | bytes 17301504 | tf_op jit(solution)/shard_map/reduce_sum | solution.py:72
  422.1 10.9 %all_gather.7 = f32[5,16384]{1,0:T(8,128)S(1)} all-gather(f32[5,2048]{1,0:T(8,128)S(1)} %subtract_divide_fusion.1), channel_id=1, replica_groups=mesh['wide'=4,'narrow'=8] {'narrow'}, dimensions={1}, use_global_device_ids=true | all-gather | bytes 368640 | tf_op jit(solution)/shard_map/all_gather | solution.py:68
  433.0 5.5 copy.52
  438.5 11.0 %gather_fusion.2 = f32[2048,5]{1,0:T(8,128)} fusion(f32[5,16384]{0,1:T(8,128)} %copy.52, s32[2048]{0:T(1024)S(1)} %broadcast_clamp_fusion.1), kind=kCustom, calls=%fused_computation.2.clone | custom fusion | bytes 90112 | tf_op jit(solution)/shard_map/jit(_take)/gather | solution.py:69
  449.4 1.6 select_bitcast_fusion.1
  452.0 4.2 mul.380
  456.1 6.2 %mul.381 = f32[5,131072]{1,0:T(8,128)} reshape(f32[5,2048,64]{2,1,0:T(8,128)} %mul.380) | data formatting | bytes 5242880 | tf_op jit(solution)/shard_map/mul | solution.py:71
  462.3 5.1 multiply_reduce_fusion.8
  467.4 1.6 multiply_reduce_fusion.10
  470.7 8.2 %multiply_reduce_fusion = f32[16,2048]{1,0:T(8,128)S(1)} fusion(f32[16,2048,64]{2,1,0:T(8,128)} %reshape.145, f32[2048,64]{1,0:T(8,128)S(1)} %multiply_subtract_fusion), kind=kLoop, calls=%fused_computation.10 | loop fusion | flops 4161536 | bytes 9043968 | tf_op jit(solution)/shard_map/reduce_sum | solution.py:31
  479.3 11.7 %scatter_custom_fusion.5 = f32[16,1024]{0,1:T(8,128)S(1)} fusion(s32[2048]{0:T(1024)} %copy-done.7, f32[2048,16]{1,0:T(8,128)S(1)} %copy.58, f32[]{:T(128)} %constant.27.clone.1), kind=kCustom, calls=%fused_computation.39 | custom fusion | flops 32768 | bytes 66048 | tf_op jit(solution)/shard_map/scatter-add | solution.py:33
  491.9 3.9 multiply_reduce_fusion.5
  496.2 15.6 %scatter_custom_fusion.4 = f32[5,16384]{0,1:T(8,128)} fusion(s32[2048]{0:T(1024)} %copy-done.8, f32[2048,5]{1,0:T(8,128)S(1)} %copy.56, f32[]{:T(128)} %constant.27.clone.1), kind=kCustom, calls=%fused_computation.20 | custom fusion | flops 10240 | bytes 328192 | tf_op jit(solution)/shard_map/scatter-add | solution.py:36
  511.7 6.0 copy.57
  518.0 7.4 %all-reduce.11.cloned.1.call-done = f32[16,1024]{1,0:T(8,128)} async-done(((f32[16,1024]{1,0:T(8,128)}), f32[16,1024]{1,0:T(8,128)}) %all-reduce.11.cloned.1.call-update) | async-done | bytes 65552 | tf_op jit(solution)/shard_map/psum | solution.py:35
  528.8 22.3 %reduce-scatter.8.cloned.1.call-done = f32[5,2048]{1,0:T(8,128)} async-done(((f32[5,16384]{1,0:T(8,128)}), f32[5,2048]{1,0:T(8,128)}) %reduce-scatter.8.cloned.1.call-update) | async-done | bytes 40976 | tf_op jit(solution)/shard_map/reduce_scatter | solution.py:37
  554.5 39.6 %all-reduce = (f32[]{:T(128)}, f32[]{:T(128)}, f32[]{:T(128)}, f32[]{:T(128)}) all-reduce(f32[]{:T(128)} %get-tuple-element.40, f32[]{:T(128)S(6)} %add.146, f32[]{:T(128)S(6)} %add.147, f32[]{:T(128)S(6)} %add.148), channel_id=1, replica_groups=mesh['wide'=4,'narrow'=8] {'wide','narrow'}, use_global_device_ids=true, to_apply=%region_33.36 | all-reduce | flops 4 | bytes 32 | tf_op jit(solution)/shard_map/psum | solution.py:46
  (80 shorter events, 35.7 us)
Async XLA Ops:
  8.0 77.6 %all-reduce.7.cloned.1.call-start = ((), (), s32[]{:S(2)}) async-start(), calls=%async_computation.4 | async-start | bytes 131072 | tf_op jit(solution)/shard_map/psum | solution.py:35
  8.0 17.4 %copy-start = (f32[131072]{0:T(1024)S(1)}, f32[131072]{0:T(1024)}, u32[]{:S(2)}) copy-start(f32[131072]{0:T(1024)} %param.12) | copy-start | bytes 1572868
  8.1 17.6 %copy-start.6 = (s32[2048]{0:T(1024)S(1)}, s32[2048]{0:T(1024)}, u32[]{:S(2)}) copy-start(s32[2048]{0:T(1024)} %param.15) | copy-start | bytes 24580
  26.0 9.6 %copy-start.10 = (s32[2048]{0:T(1024)S(1)}, s32[2048]{0:T(1024)}, u32[]{:S(2)}) copy-start(s32[2048]{0:T(1024)} %param.14) | copy-start | bytes 24580
  35.6 225.2 %copy-start.7 = (s32[2048]{0:T(1024)}, s32[2048]{0:T(1024)S(1)}, u32[]{:S(2)}) copy-start(s32[2048]{0:T(1024)S(1)} %get-tuple-element.45) | copy-start | bytes 24580
  35.7 23.6 %copy-start.11 = (s32[2048]{0:T(1024)S(1)}, s32[2048]{0:T(1024)}, u32[]{:S(2)}) copy-start(s32[2048]{0:T(1024)} %param.13) | copy-start | bytes 24580
  48.5 69.3 %reduce-scatter.4.cloned.1.call-start = ((), (), s32[]{:S(2)}) async-start(), calls=%async_computation.3 | async-start | bytes 589824 | tf_op jit(solution)/shard_map/reduce_scatter | solution.py:37
  59.3 129.9 %copy-start.9 = (pred[2048]{0:T(1024)(128)(4,1)}, pred[2048]{0:T(1024)(128)(4,1)S(1)}, u32[]{:S(2)}) copy-start(pred[2048]{0:T(1024)(128)(4,1)S(1)} %get-tuple-element.46) | copy-start | bytes 6148
  59.3 218.7 %copy-start.8 = (s32[2048]{0:T(1024)}, s32[2048]{0:T(1024)S(1)}, u32[]{:S(2)}) copy-start(s32[2048]{0:T(1024)S(1)} %get-tuple-element.47) | copy-start | bytes 24580
  80.9 226.2 %all-reduce.9.cloned.1.call-start = ((), (), s32[]{:S(2)}) async-start(), calls=%async_computation.6 | async-start | bytes 131072 | tf_op jit(solution)/shard_map/psum | solution.py:35
  194.5 11.9 %copy-start.3 = (f32[16,1024]{1,0:T(8,128)S(1)}, f32[16,1024]{1,0:T(8,128)}, u32[]{:S(2)}) copy-start(f32[16,1024]{1,0:T(8,128)} %all-reduce.7.cloned.1.call-done) | copy-start | bytes 196612
  239.9 7.6 %copy-start.1 = (f32[131072]{0:T(1024)S(1)}, f32[131072]{0:T(1024)}, u32[]{:S(2)}) copy-start(f32[131072]{0:T(1024)} %multiply_reduce_fusion.9) | copy-start | bytes 1572868
  273.6 58.8 %reduce-scatter.6.cloned.1.call-start = ((), (), s32[]{:S(2)}) async-start(), calls=%async_computation.5 | async-start | bytes 589824 | tf_op jit(solution)/shard_map/reduce_scatter | solution.py:37
  278.0 54.5 %copy-start.4 = (f32[5,2048]{1,0:T(8,128)S(1)}, f32[5,2048]{1,0:T(8,128)}, u32[]{:S(2)}) copy-start(f32[5,2048]{1,0:T(8,128)} %reduce-scatter.4.cloned.1.call-done) | copy-start | bytes 122884
  299.2 226.2 %all-reduce.11.cloned.1.call-start = ((), (), s32[]{:S(2)}) async-start(), calls=%async_computation.8 | async-start | bytes 131072 | tf_op jit(solution)/shard_map/psum | solution.py:35
  413.9 8.2 %copy-start.5 = (f32[5,2048]{1,0:T(8,128)S(1)}, f32[5,2048]{1,0:T(8,128)}, u32[]{:S(2)}) copy-start(f32[5,2048]{1,0:T(8,128)} %reduce-scatter.6.cloned.1.call-done) | copy-start | bytes 122884
  456.1 11.2 %copy-start.2 = (f32[131072]{0:T(1024)S(1)}, f32[131072]{0:T(1024)}, u32[]{:S(2)}) copy-start(f32[131072]{0:T(1024)} %multiply_reduce_fusion.3) | copy-start | bytes 1572868
  491.8 59.2 %reduce-scatter.8.cloned.1.call-start = ((), (), s32[]{:S(2)}) async-start(), calls=%async_computation.7 | async-start | bytes 589824 | tf_op jit(solution)/shard_map/reduce_scatter | solution.py:37
Sparse Core Ops, SparseCore 0:
  48.6 37.0 all-reduce.6
  273.7 33.3 all-reduce.8
  492.0 33.3 all-reduce.10
Sparse Core Ops, SparseCore 1:
  81.0 36.8 reduce-scatter.3
  299.3 33.1 reduce-scatter.5
  517.8 33.1 reduce-scatter.7
where the time goes:
time: 616 us; the launch traced here: 608 us
  local copies, waits for them, and re-layouts  171 us (28%)
  other arithmetic  171 us (28%)
  blocking collectives  140 us (23%)
  waiting for transfers between devices  92.8 us (15%)
  between operations  32.3 us (5%)
    psum x3, blocking collectives, merged_total(): return lax.psum((first, second, third, fourth), ('wide', 'narrow'))  119 us
    reduce_scatter x3, waiting for transfers between devices, transposed(): lax.psum_scatter(src_total, 'narrow', scatter_dimension=1, tiled=True)  74.2 us
    mul x4, local copies, waits for them, and re-layouts, on_device(): image = image + jnp.sum(att_blocks * att_vals[:, :, None], axis=0)  48.4 us
    scatter-add x3, other arithmetic, transposed(): jnp.zeros((param_rows, group_size), jnp.float32).at[:, src_index]  45.9 us
    scatter-add x3, other arithmetic, transposed(): jnp.zeros((att_blocks.shape[0], SEG_DEV), jnp.float32).at[:, seg_index]  35.6 us
    reduce_sum x3, other arithmetic, transposed(): att_part = jnp.sum(att_blocks * obs_vec[None], axis=2)  24.9 us
    gather x2, local copies, waits for them, and re-layouts, on_device(): src_vals = jnp.take(whole_src, src_index, axis=1)  21.9 us
    all_gather x2, blocking collectives, on_device(): whole_src = lax.all_gather(src_vec, 'narrow', axis=1, tiled=True)  21.7 us
  transfers between devices with their start and end apart: 6, of which 6 were waited for; matrix products, arithmetic and copies ran while one was open for 15% of the time, Pallas kernels for 0%

commit v1 on v0

--- a/solution.py
+++ b/solution.py
@@ -6,6 +6,24 @@
 ITERS = 2
 SRC_DEV = 2048
 SEG_DEV = 1024
+
+
+def in_order(pieces, dim):
+    pieces = jnp.moveaxis(pieces, 0, dim)
+    shape = pieces.shape
+    return pieces.reshape(*shape[:dim], shape[dim] * shape[dim + 1], *shape[dim + 2 :])
+
+
+def doubled(x, axis):
+    peers = lax.axis_size(axis)
+    parts = x[None]
+    for level in range(peers.bit_length() - 1):
+        stride = 1 << level
+        received = lax.ppermute(parts, axis, [(i, i ^ stride) for i in range(peers)])
+        both = jnp.stack([parts, received])
+        upper = lax.axis_index(axis) >> level & 1
+        parts = jnp.where(upper == 0, both, both[::-1]).reshape(-1, *x.shape)
+    return parts
 
 
 def on_device(src_design, att_design, right_side, block_source, block_segment, block_count):
@@ -65,7 +83,7 @@
     phi_bar = beta_norm
     rho_bar = alpha_norm
     for step in range(ITERS):
-        whole_src = lax.all_gather(src_vec, "narrow", axis=1, tiled=True)
+        whole_src = in_order(doubled(src_vec, "narrow"), 1)
         src_vals = jnp.take(whole_src, src_index, axis=1)
         att_vals = jnp.take(att_vec, seg_index, axis=1)
         image = jnp.sum(src_blocks * src_vals[:, :, None], axis=0)

time: 616 us -> 728 us (1.18)
  waiting for transfers between devices: 92.8 us -> 202 us
  blocking collectives: 140 us -> 119 us
  other arithmetic: 171 us -> 184 us
  starting transfers between devices: 0.46 us -> 8.9 us
    reduce_scatter x3, waiting for transfers between devices: 74.2 us -> 168 us  [transposed(): lax.psum_scatter(src_total, 'narrow', scatter_dimension=1, tiled=True)]
    all_gather x2 -> x0, blocking collectives: 21.7 us -> none  [on_device(): whole_src = lax.all_gather(src_vec, 'narrow', axis=1, tiled=True)]
    scatter-add x3 -> x0, local copies, waits for them, and re-layouts: 18 us -> none  [transposed(): jnp.zeros((param_rows, group_size), jnp.float32).at[:, src_index]]
    psum x3, waiting for transfers between devices: 18.5 us -> 34.5 us  [transposed(): att_vec = lax.psum(att_total, 'wide')]
    all_gather x2 -> x0, local copies, waits for them, and re-layouts: 11.2 us -> none  [on_device(): whole_src = lax.all_gather(src_vec, 'narrow', axis=1, tiled=True)]
    transpose x0 -> x2, local copies, waits for them, and re-layouts: none -> 10.5 us  [in_order(): pieces = jnp.moveaxis(pieces, 0, dim)]
    ppermute x0 -> x6, starting transfers between devices: none -> 8.22 us  [doubled(): lax.ppermute(parts, axis, [(i, i ^ stride) for i in range(peers)])]
  transfers between devices with their start and end apart: 6 -> 12, of which waited for: 6 -> 6; matrix products, arithmetic and copies ran while one was open for 15% -> 22% of each run, Pallas kernels for 0% -> 0%
where the time goes in v1:
time: 728 us; the launch traced here: 720 us
  waiting for transfers between devices  202 us (28%)
  other arithmetic  184 us (25%)
  local copies, waits for them, and re-layouts  172 us (24%)
  blocking collectives  119 us (16%)
  between operations  32.7 us (4%)
  starting transfers between devices  8.9 us (1%)
    reduce_scatter x3, waiting for transfers between devices, transposed(): lax.psum_scatter(src_total, 'narrow', scatter_dimension=1, tiled=True)  168 us
    psum x3, blocking collectives, merged_total(): return lax.psum((first, second, third, fourth), ('wide', 'narrow'))  119 us
    mul x4, local copies, waits for them, and re-layouts, on_device(): image = image + jnp.sum(att_blocks * att_vals[:, :, None], axis=0)  47.6 us
    scatter-add x3, other arithmetic, transposed(): jnp.zeros((param_rows, group_size), jnp.float32).at[:, src_index]  45.6 us
    scatter-add x3, other arithmetic, transposed(): jnp.zeros((att_blocks.shape[0], SEG_DEV), jnp.float32).at[:, seg_index]  35.5 us
    psum x3, waiting for transfers between devices, transposed(): att_vec = lax.psum(att_total, 'wide')  34.5 us
    reduce_sum x3, other arithmetic, transposed(): att_part = jnp.sum(att_blocks * obs_vec[None], axis=2)  25.1 us
    gather x2, local copies, waits for them, and re-layouts, on_device(): src_vals = jnp.take(whole_src, src_index, axis=1)  21.9 us
  transfers between devices with their start and end apart: 12, of which 6 were waited for; matrix products, arithmetic and copies ran while one was open for 22% of the time, Pallas kernels for 0%

profile of v1, /device:TPU:0, one launch (start us, length us, event | category | flops | bytes accessed | tf_op | source)
XLA Modules:
  0.0 719.7 jit_solution(10501464689899645234)
XLA Ops:
  8.1 17.4 %reshape.169 = f32[16,2048,64]{2,1,0:T(8,128)} reshape(f32[16,131072]{1,0:T(8,128)} %param.11) | data formatting | bytes 16777216 | tf_op jit(solution)/shard_map/reshape | solution.py:38
  26.1 8.2 %multiply_reduce_fusion.2 = f32[16,2048]{1,0:T(8,128)S(1)} fusion(f32[16,2048,64]{2,1,0:T(8,128)} %reshape.169, f32[2048,64]{1,0:T(8,128)S(1)} %fusion.6), kind=kLoop, calls=%fused_computation.12 | loop fusion | flops 4161536 | bytes 9043968 | tf_op jit(solution)/shard_map/reduce_sum | solution.py:49
  35.7 12.0 %scatter_custom_fusion.1 = f32[16,1024]{0,1:T(8,128)S(1)} fusion(s32[2048]{0:T(1024)S(1)} %get-tuple-element.53, f32[2048,16]{1,0:T(8,128)} %copy.75, f32[]{:T(128)} %constant.27.clone.1), kind=kCustom, calls=%fused_computation.59 | custom fusion | flops 32768 | bytes 66048 | tf_op jit(solution)/shard_map/scatter-add | solution.py:51
  48.7 6.6 reshape.167
  55.3 3.9 multiply_reduce_fusion.7
  59.7 15.2 %scatter_custom_fusion = f32[5,16384]{0,1:T(8,128)} fusion(s32[2048]{0:T(1024)S(1)} %get-tuple-element.55, f32[2048,5]{1,0:T(8,128)S(1)} %copy.74, f32[]{:T(128)} %constant.27.clone.1), kind=kCustom, calls=%fused_computation.24 | custom fusion | flops 10240 | bytes 327684 | tf_op jit(solution)/shard_map/scatter-add | solution.py:54
  76.3 9.3 %all-reduce.7.cloned.1.call-done = f32[16,1024]{1,0:T(8,128)} async-done(((f32[16,1024]{1,0:T(8,128)}), f32[16,1024]{1,0:T(8,128)}) %all-reduce.7.cloned.1.call-update) | async-done | bytes 65552 | tf_op jit(solution)/shard_map/psum | solution.py:53
  87.8 61.2 %reduce-scatter.4.cloned.1.call-done = f32[5,2048]{0,1:T(8,128)} async-done(((f32[5,16384]{0,1:T(8,128)}), f32[5,2048]{0,1:T(8,128)}) %reduce-scatter.4.cloned.1.call-update) | async-done | bytes 40976 | tf_op jit(solution)/shard_map/reduce_scatter | solution.py:55
  151.8 40.0 %all-reduce.2 = (f32[]{:T(128)}, f32[]{:T(128)}) all-reduce(f32[]{:T(128)} %multiply_reduce_fusion.19, f32[]{:T(128)S(6)} %add.133), channel_id=1, replica_groups=mesh['wide'=4,'narrow'=8] {'wide','narrow'}, use_global_device_ids=true, to_apply=%region_10.0 | all-reduce | flops 2 | bytes 16 | tf_op jit(solution)/shard_map/psum | solution.py:64
  193.2 2.4 fusion.18
  198.6 7.6 %gather_fusion.1 = f32[2048,16]{1,0:T(8,128)} fusion(f32[16,1024]{0,1:T(8,128)S(1)} %copy.84, s32[2048]{0:T(1024)S(1)} %broadcast_clamp_fusion), kind=kCustom, calls=%fused_computation.1.clone | custom fusion | bytes 270336 | tf_op jit(solution)/shard_map/jit(_take)/gather | solution.py:88
  206.9 2.3 collective-permute-start.1
  211.1 8.3 %mul.348 = f32[16,2048,64]{2,1,0:T(8,128)} broadcast(f32[16,2048]{1,0:T(8,128)S(1)} %copy.85), dimensions={0,1} | broadcast | bytes 8519680 | tf_op jit(solution)/shard_map/mul | solution.py:90
  219.4 15.5 %mul.349 = f32[16,131072]{1,0:T(8,128)} reshape(f32[16,2048,64]{2,1,0:T(8,128)} %mul.348) | data formatting | bytes 16777216 | tf_op jit(solution)/shard_map/mul | solution.py:90
  237.0 7.5 %multiply_reduce_fusion.4 = f32[131072]{0:T(1024)S(1)} fusion(f32[16,131072]{1,0:T(8,128)} %param.11, f32[16,131072]{1,0:T(8,128)} %mul.349), kind=kLoop, calls=%fused_computation.14 | loop fusion | flops 4063232 | bytes 17301504 | tf_op jit(solution)/shard_map/reduce_sum | solution.py:90
  245.0 4.7 copy.82
  249.6 11.0 %gather_fusion = f32[2048,5]{1,0:T(8,128)} fusion(f32[5,16384]{0,1:T(8,128)} %bitcast.53, s32[2048]{0:T(1024)S(1)} %broadcast_clamp_fusion.1), kind=kCustom, calls=%fused_computation.clone | custom fusion | bytes 90112 | tf_op jit(solution)/shard_map/jit(_take)/gather | solution.py:87
  262.5 3.6 mul.345
  266.1 6.1 mul.346
  272.2 5.1 multiply_reduce_fusion.9
  280.7 8.2 %multiply_reduce_fusion.1 = f32[16,2048]{1,0:T(8,128)S(1)} fusion(f32[16,2048,64]{2,1,0:T(8,128)} %reshape.169, f32[2048,64]{1,0:T(8,128)S(1)} %multiply_subtract_fusion.3), kind=kLoop, calls=%fused_computation.11 | loop fusion | flops 4161536 | bytes 9043968 | tf_op jit(solution)/shard_map/reduce_sum | solution.py:49
  289.3 11.6 %scatter_custom_fusion.3 = f32[16,1024]{0,1:T(8,128)S(1)} fusion(s32[2048]{0:T(1024)S(1)} %get-tuple-element.53, f32[2048,16]{1,0:T(8,128)S(1)} %copy.87, f32[]{:T(128)} %constant.27.clone.1), kind=kCustom, calls=%fused_computation.57 | custom fusion | flops 32768 | bytes 65540 | tf_op jit(solution)/shard_map/scatter-add | solution.py:51
  301.8 3.9 multiply_reduce_fusion.6
  306.1 15.2 %scatter_custom_fusion.2 = f32[5,16384]{0,1:T(8,128)} fusion(s32[2048]{0:T(1024)S(1)} %get-tuple-element.55, f32[2048,5]{1,0:T(8,128)S(1)} %copy.86, f32[]{:T(128)} %constant.27.clone.1), kind=kCustom, calls=%fused_computation.22 | custom fusion | flops 10240 | bytes 327684 | tf_op jit(solution)/shard_map/scatter-add | solution.py:54
  321.6 12.8 %all-reduce.9.cloned.1.call-done = f32[16,1024]{1,0:T(8,128)} async-done(((f32[16,1024]{1,0:T(8,128)}), f32[16,1024]{1,0:T(8,128)}) %all-reduce.9.cloned.1.call-update) | async-done | bytes 65552 | tf_op jit(solution)/shard_map/psum | solution.py:53
  337.8 53.1 %reduce-scatter.6.cloned.1.call-done = f32[5,2048]{0,1:T(8,128)} async-done(((f32[5,16384]{0,1:T(8,128)}), f32[5,2048]{0,1:T(8,128)}) %reduce-scatter.6.cloned.1.call-update) | async-done | bytes 40976 | tf_op jit(solution)/shard_map/reduce_scatter | solution.py:55
  395.1 39.6 %all-reduce.1 = (f32[]{:T(128)}, f32[]{:T(128)}, f32[]{:T(128)}, f32[]{:T(128)}) all-reduce(f32[]{:T(128)S(6)} %add.137, f32[]{:T(128)} %get-tuple-element.50, f32[]{:T(128)S(6)} %add.138, f32[]{:T(128)S(6)} %add.139), channel_id=1, replica_groups=mesh['wide'=4,'narrow'=8] {'wide','narrow'}, use_global_device_ids=true, to_apply=%region_23.26 | all-reduce | flops 4 | bytes 32 | tf_op jit(solution)/shard_map/psum | solution.py:64
  441.0 8.6 %gather_fusion.3 = f32[2048,16]{1,0:T(8,128)} fusion(f32[16,1024]{0,1:T(8,128)} %copy.96, s32[2048]{0:T(1024)S(1)} %broadcast_clamp_fusion), kind=kCustom, calls=%fused_computation.3.clone | custom fusion | bytes 270336 | tf_op jit(solution)/shard_map/jit(_take)/gather | solution.py:88
  451.2 5.8 rev.21
  458.6 2.3 collective-permute-start.4
  460.9 2.6 select_bitcast_fusion
  464.9 8.3 %mul.384 = f32[16,2048,64]{2,1,0:T(8,128)} broadcast(f32[16,2048]{1,0:T(8,128)S(1)} %copy.97), dimensions={0,1} | broadcast | bytes 8519680 | tf_op jit(solution)/shard_map/mul | solution.py:90
  473.3 15.5 %mul.385 = f32[16,131072]{1,0:T(8,128)} reshape(f32[16,2048,64]{2,1,0:T(8,128)} %mul.384) | data formatting | bytes 16777216 | tf_op jit(solution)/shard_map/mul | solution.py:90
  492.4 8.3 %multiply_reduce_fusion.3 = f32[131072]{0:T(1024)} fusion(f32[16,131072]{1,0:T(8,128)} %param.11, f32[16,131072]{1,0:T(8,128)} %mul.385), kind=kLoop, calls=%fused_computation.13 | loop fusion | flops 4063232 | bytes 17301504 | tf_op jit(solution)/shard_map/reduce_sum | solution.py:90
  505.2 5.8 copy.94
  511.0 11.0 %gather_fusion.2 = f32[2048,5]{1,0:T(8,128)} fusion(f32[5,16384]{0,1:T(8,128)} %bitcast.52, s32[2048]{0:T(1024)S(1)} %broadcast_clamp_fusion.1), kind=kCustom, calls=%fused_computation.2.clone | custom fusion | bytes 90112 | tf_op jit(solution)/shard_map/jit(_take)/gather | solution.py:87
  521.9 2.6 select_bitcast_fusion.1
  526.1 3.7 mul.380
  529.8 6.1 mul.381
  535.9 5.3 multiply_reduce_fusion.8
  546.7 8.6 %multiply_reduce_fusion = f32[16,2048]{1,0:T(8,128)S(1)} fusion(f32[16,2048,64]{2,1,0:T(8,128)} %reshape.169, f32[2048,64]{1,0:T(8,128)S(1)} %multiply_subtract_fusion.1), kind=kLoop, calls=%fused_computation.10 | loop fusion | flops 4161536 | bytes 9043968 | tf_op jit(solution)/shard_map/reduce_sum | solution.py:49
  556.6 11.9 %scatter_custom_fusion.5 = f32[16,1024]{0,1:T(8,128)S(1)} fusion(s32[2048]{0:T(1024)} %copy-done.14, f32[2048,16]{1,0:T(8,128)} %copy.99, f32[]{:T(128)} %constant.27.clone.1), kind=kCustom, calls=%fused_computation.55 | custom fusion | flops 32768 | bytes 66048 | tf_op jit(solution)/shard_map/scatter-add | solution.py:51
  569.4 4.2 multiply_reduce_fusion.5
  574.0 15.3 %scatter_custom_fusion.4 = f32[5,16384]{0,1:T(8,128)} fusion(s32[2048]{0:T(1024)} %copy-done.15, f32[2048,5]{1,0:T(8,128)S(1)} %copy.98, f32[]{:T(128)} %constant.27.clone.1), kind=kCustom, calls=%fused_computation.20 | custom fusion | flops 10240 | bytes 328192 | tf_op jit(solution)/shard_map/scatter-add | solution.py:54
  589.6 12.4 %all-reduce.11.cloned.1.call-done = f32[16,1024]{1,0:T(8,128)} async-done(((f32[16,1024]{1,0:T(8,128)}), f32[16,1024]{1,0:T(8,128)}) %all-reduce.11.cloned.1.call-update) | async-done | bytes 65552 | tf_op jit(solution)/shard_map/psum | solution.py:53
  605.4 53.5 %reduce-scatter.8.cloned.1.call-done = f32[5,2048]{0,1:T(8,128)} async-done(((f32[5,16384]{0,1:T(8,128)}), f32[5,2048]{0,1:T(8,128)}) %reduce-scatter.8.cloned.1.call-update) | async-done | bytes 40976 | tf_op jit(solution)/shard_map/reduce_scatter | solution.py:55
  663.0 39.6 %all-reduce = (f32[]{:T(128)}, f32[]{:T(128)}, f32[]{:T(128)}, f32[]{:T(128)}) all-reduce(f32[]{:T(128)} %get-tuple-element.48, f32[]{:T(128)S(6)} %add.146, f32[]{:T(128)S(6)} %add.147, f32[]{:T(128)S(6)} %add.148), channel_id=1, replica_groups=mesh['wide'=4,'narrow'=8] {'wide','narrow'}, use_global_device_ids=true, to_apply=%region_33.36 | all-reduce | flops 4 | bytes 32 | tf_op jit(solution)/shard_map/psum | solution.py:64
  705.5 2.7 multiply_subtract_fusion
  (133 shorter events, 61.1 us)
Async XLA Ops:
  8.0 77.6 %all-reduce.7.cloned.1.call-start = ((), (), s32[]{:S(2)}) async-start(), calls=%async_computation.4 | async-start | bytes 131072 | tf_op jit(solution)/shard_map/psum | solution.py:53
  8.0 17.4 %copy-start.2 = (f32[131072]{0:T(1024)S(1)}, f32[131072]{0:T(1024)}, u32[]{:S(2)}) copy-start(f32[131072]{0:T(1024)} %param.12) | copy-start | bytes 1572868
  8.1 17.6 %copy-start.13 = (s32[2048]{0:T(1024)S(1)}, s32[2048]{0:T(1024)}, u32[]{:S(2)}) copy-start(s32[2048]{0:T(1024)} %param.15) | copy-start | bytes 24580
  26.1 9.6 %copy-start.18 = (s32[2048]{0:T(1024)S(1)}, s32[2048]{0:T(1024)}, u32[]{:S(2)}) copy-start(s32[2048]{0:T(1024)} %param.14) | copy-start | bytes 24580
  35.7 253.6 %copy-start.14 = (s32[2048]{0:T(1024)}, s32[2048]{0:T(1024)S(1)}, u32[]{:S(2)}) copy-start(s32[2048]{0:T(1024)S(1)} %get-tuple-element.53) | copy-start | bytes 24580
  35.7 23.6 %copy-start.19 = (s32[2048]{0:T(1024)S(1)}, s32[2048]{0:T(1024)}, u32[]{:S(2)}) copy-start(s32[2048]{0:T(1024)} %param.13) | copy-start | bytes 24580
  48.5 100.5 %reduce-scatter.4.cloned.1.call-start = ((), (), s32[]{:S(2)}) async-start(), calls=%async_computation.3 | async-start | bytes 9437184 | tf_op jit(solution)/shard_map/reduce_scatter | solution.py:55
  59.3 201.3 %copy-start.16 = (pred[2048]{0:T(1024)(128)(4,1)}, pred[2048]{0:T(1024)(128)(4,1)S(1)}, u32[]{:S(2)}) copy-start(pred[2048]{0:T(1024)(128)(4,1)S(1)} %get-tuple-element.54) | copy-start | bytes 6148
  59.3 246.8 %copy-start.15 = (s32[2048]{0:T(1024)}, s32[2048]{0:T(1024)S(1)}, u32[]{:S(2)}) copy-start(s32[2048]{0:T(1024)S(1)} %get-tuple-element.55) | copy-start | bytes 24580
  74.9 259.5 %all-reduce.9.cloned.1.call-start = ((), (), s32[]{:S(2)}) async-start(), calls=%async_computation.6 | async-start | bytes 131072 | tf_op jit(solution)/shard_map/psum | solution.py:53
  197.1 9.0 %collective-permute-start = (f32[1,5,2048]{2,0,1:T(1,128)S(1)}, f32[1,5,2048]{2,0,1:T(1,128)S(1)}, u32[]{:S(2)}, u32[]{:S(2)}) collective-permute-start(f32[1,5,2048]{2,0,1:T(1,128)S(1)} %copy.77), channel_id=1, source_target_pairs={{0,1},{1,0},{2,3},{3,2},{4,5},{5,4},{6,7},{7,6},{8,9},{9,8},{10,11... | collective-permute-start | bytes 122888 | tf_op jit(solution)/shard_map/ppermute | solution.py:22
  206.9 28.0 %collective-permute-start.1 = (f32[2,5,2048]{2,0,1:T(2,128)S(1)}, f32[2,5,2048]{2,0,1:T(2,128)S(1)}, u32[]{:S(2)}, u32[]{:S(2)}) collective-permute-start(f32[2,5,2048]{2,0,1:T(2,128)S(1)} %get-tuple-element.63), channel_id=1, source_target_pairs={{0,2},{1,3},{2,0},{3,1},{4,6},{5,7},{6,4},{7,5},{8,10},{9,11},{10,... | collective-permute-start | bytes 245768 | tf_op jit(solution)/shard_map/ppermute | solution.py:22
  235.3 9.4 %collective-permute-start.2 = (f32[4,5,2048]{2,0,1:T(4,128)S(1)}, f32[4,5,2048]{2,0,1:T(4,128)S(1)}, u32[]{:S(2)}, u32[]{:S(2)}) collective-permute-start(f32[4,5,2048]{2,0,1:T(4,128)S(1)} %reshape.171), channel_id=1, source_target_pairs={{0,4},{1,5},{2,6},{3,7},{4,0},{5,1},{6,2},{7,3},{8,12},{9,13},{10,... | collective-permute-start | bytes 491528 | tf_op jit(solution)/shard_map/ppermute | solution.py:22
  278.0 10.9 %copy-start.4 = (f32[131072]{0:T(1024)}, f32[131072]{0:T(1024)S(1)}, u32[]{:S(2)}) copy-start(f32[131072]{0:T(1024)S(1)} %get-tuple-element.51) | copy-start | bytes 1572868
  301.7 89.2 %reduce-scatter.6.cloned.1.call-start = ((), (), s32[]{:S(2)}) async-start(), calls=%async_computation.5 | async-start | bytes 9437184 | tf_op jit(solution)/shard_map/reduce_scatter | solution.py:55
  306.1 28.3 %copy-start.7 = (f32[16,1024]{1,0:T(8,128)S(1)}, f32[16,1024]{1,0:T(8,128)}, u32[]{:S(2)}) copy-start(f32[16,1024]{1,0:T(8,128)} %all-reduce.7.cloned.1.call-done) | copy-start | bytes 196612
  306.1 84.8 %copy-start = (f32[5,2048]{0,1:T(8,128)S(1)}, f32[5,2048]{0,1:T(8,128)}, u32[]{:S(2)}) copy-start(f32[5,2048]{0,1:T(8,128)} %reduce-scatter.4.cloned.1.call-done) | copy-start | bytes 122884
  321.3 280.6 %all-reduce.11.cloned.1.call-start = ((), (), s32[]{:S(2)}) async-start(), calls=%async_computation.8 | async-start | bytes 131072 | tf_op jit(solution)/shard_map/psum | solution.py:53
  439.0 10.9 %collective-permute-start.3 = (f32[1,5,2048]{2,0,1:T(1,128)S(1)}, f32[1,5,2048]{2,0,1:T(1,128)S(1)}, u32[]{:S(2)}, u32[]{:S(2)}) collective-permute-start(f32[1,5,2048]{2,0,1:T(1,128)S(1)} %copy.89), channel_id=1, source_target_pairs={{0,1},{1,0},{2,3},{3,2},{4,5},{5,4},{6,7},{7,6},{8,9},{9,8},{10,11... | collective-permute-start | bytes 122888 | tf_op jit(solution)/shard_map/ppermute | solution.py:22
  439.9 33.3 %copy-start.8 = (f32[16,1024]{1,0:T(8,128)}, f32[16,1024]{1,0:T(8,128)S(1)}, u32[]{:S(2)}) copy-start(f32[16,1024]{1,0:T(8,128)S(1)} %subtract_divide_fusion.1) | copy-start | bytes 196612
  449.9 0.6 copy-start.12
  458.6 30.2 %collective-permute-start.4 = (f32[2,5,2048]{2,0,1:T(2,128)}, f32[2,5,2048]{2,0,1:T(2,128)}, u32[]{:S(2)}, u32[]{:S(2)}) collective-permute-start(f32[2,5,2048]{2,0,1:T(2,128)} %get-tuple-element.61), channel_id=1, source_target_pairs={{0,2},{1,3},{2,0},{3,1},{4,6},{5,7},{6,4},{7,5},{8,10},{9,11},{10,... | collective-permute-start | bytes 245768 | tf_op jit(solution)/shard_map/ppermute | solution.py:22
  473.3 15.5 %copy-start.10 = (f32[1,2,5,2048]{3,1,2,0:T(2,128)S(1)}, f32[1,2,5,2048]{3,1,2,0:T(2,128)}, u32[]{:S(2)}) copy-start(f32[1,2,5,2048]{3,1,2,0:T(2,128)} %get-tuple-element.60) | copy-start | bytes 245764
  490.6 10.8 %collective-permute-start.5 = (f32[4,5,2048]{2,0,1:T(4,128)}, f32[4,5,2048]{2,0,1:T(4,128)}, u32[]{:S(2)}, u32[]{:S(2)}) collective-permute-start(f32[4,5,2048]{2,0,1:T(4,128)} %reshape.175), channel_id=1, source_target_pairs={{0,4},{1,5},{2,6},{3,7},{4,0},{5,1},{6,2},{7,3},{8,12},{9,13},{10,... | collective-permute-start | bytes 491528 | tf_op jit(solution)/shard_map/ppermute | solution.py:22
  500.6 21.3 %copy-start.17 = (pred[2048]{0:T(1024)(128)(4,1)S(1)}, pred[2048]{0:T(1024)(128)(4,1)}, u32[]{:S(2)}) copy-start(pred[2048]{0:T(1024)(128)(4,1)} %copy-done.16) | copy-start | bytes 6148
  535.9 5.3 copy-start.3
  535.9 5.3 copy-start.5
  535.9 5.3 copy-start.6
  546.7 8.6 %copy-start.1 = (f32[2048,64]{1,0:T(8,128)}, f32[2048,64]{1,0:T(8,128)S(1)}, u32[]{:S(2)}) copy-start(f32[2048,64]{1,0:T(8,128)S(1)} %multiply_subtract_fusion.1) | copy-start | bytes 1572868
  569.4 89.5 %reduce-scatter.8.cloned.1.call-start = ((), (), s32[]{:S(2)}) async-start(), calls=%async_computation.7 | async-start | bytes 9437184 | tf_op jit(solution)/shard_map/reduce_scatter | solution.py:55
  574.0 27.9 %copy-start.9 = (f32[16,1024]{1,0:T(8,128)S(1)}, f32[16,1024]{1,0:T(8,128)}, u32[]{:S(2)}) copy-start(f32[16,1024]{1,0:T(8,128)} %copy-done.8) | copy-start | bytes 196612
  601.9 109.4 %copy-start.11 = (f32[16,1024]{1,0:T(8,128)S(1)}, f32[16,1024]{1,0:T(8,128)}, u32[]{:S(2)}) copy-start(f32[16,1024]{1,0:T(8,128)} %all-reduce.11.cloned.1.call-done) | copy-start | bytes 196612
Sparse Core Ops, SparseCore 0:
  48.6 37.0 all-reduce.6
  301.9 32.4 all-reduce.8
  569.5 32.3 all-reduce.10
Sparse Core Ops, SparseCore 1:
  74.9 74.0 reduce-scatter.3
  321.4 69.5 reduce-scatter.5
  589.4 69.4 reduce-scatter.7
